TPU v7x, 256 devices: a whole 4x4x8 slice. The times are simulated.
256 devices in a mesh: dp: 32 (over z, x), rows: 8 (over y, core).
Axes of the slice: x: 4, y: 4, z: 8, core: 2. Of those that a mesh axis runs over, the one named last changes fastest.
Arguments:
- token_ids: int32 [256, 128], P(('dp', 'rows')), may hold values from 0 to 8191, as said below
- upstream: bfloat16 [256, 128, 5376], P(('dp', 'rows')), may hold values from -6 to 6
- saved_rows: bfloat16 [256, 128, 5376], P(('dp', 'rows')), may hold values from -4 to 4
- norm_gain: float32 [5376], replicated, may hold values from 0.5 to 1.5
- master: float32 [8192, 5376], P('rows', 'dp'), may hold values from -6 to 6
- moment_one: float32 [8192, 5376], P('rows', 'dp'), may hold values from -4 to 4
- moment_two: float32 [8192, 5376], P('rows', 'dp'), may hold values from 0.1 to 4
Outputs:
- master_new: float32 [8192, 5376], P('rows', 'dp')
- moment_one_new: float32 [8192, 5376], P('rows', 'dp')
- moment_two_new: float32 [8192, 5376], P('rows', 'dp')
- new_rows: bfloat16 [256, 128, 5376], P(('dp', 'rows'))
Inputs may be any that keep to these rules, and one draw needn't show every extreme that they name: `token_ids`: rows v with v // 1024 = k belong to owner k. In each sequence, one owner receives exactly 32 of its tokens and every other owner at most 32.
All inputs are finite; a program needn't handle non-finite values.
Results may differ from a plain program's by a relative error of at most 0.007.
Values may be sent and summed in bfloat16 or wider, within the bound.
A program may use at most 64 MiB of HBM per device.

v0:
```python
import math
import jax
import jax.numpy as jnp
from jax import lax
from jax.sharding import PartitionSpec as P


def from_everyone(x, axis):
    copies = jnp.broadcast_to(x, (lax.axis_size(axis), *x.shape))
    return lax.all_to_all(copies, axis, split_axis=0, concat_axis=0, tiled=True)


def in_order(tiles, dim):
    dims = list(tiles.shape[1:])
    dims[dim] *= tiles.shape[0]
    return jnp.moveaxis(tiles, 0, dim).reshape(dims)


def collect(x, axis, dim):
    tiles = from_everyone(x, axis)
    return in_order(tiles, dim)


def norm_back(upstream_rows, saved, gain):
    values = saved.astype(jnp.float32)
    row_mean = jnp.mean(values, axis=-1, keepdims=True)
    centered = values - row_mean
    variance = jnp.mean(centered * centered, axis=-1, keepdims=True)
    inv_std = lax.rsqrt(variance + 1e-05)
    normed = centered * inv_std
    scaled = upstream_rows.astype(jnp.float32) * gain
    mean_scaled = jnp.mean(scaled, axis=-1, keepdims=True)
    mean_cross = jnp.mean(scaled * normed, axis=-1, keepdims=True)
    return (inv_std * (scaled - mean_scaled - normed * mean_cross)).astype(jnp.bfloat16)


def per_device(token_ids, upstream, saved_rows, norm_gain, master, moment_one, moment_two):
    owned_rows = master.shape[0]
    slice_width = master.shape[1]
    seq_tokens = token_ids.shape[1]
    group_ids = collect(token_ids, "dp", 0)
    row_input = norm_back(upstream[0], saved_rows[0], norm_gain)[None]
    slices = lax.all_to_all(row_input, "dp", split_axis=2, concat_axis=0, tiled=True)
    row_iota = lax.iota(jnp.int32, owned_rows)
    owners = lax.axis_size("rows")
    seq_count = slices.shape[0]
    capacity = seq_tokens // 4
    owner = group_ids // owned_rows
    local = group_ids - owner * owned_rows
    owner_hot = (owner[:, :, None] == lax.iota(jnp.int32, owners)[None, None, :]).astype(jnp.int32)
    before = jnp.cumsum(owner_hot, axis=1) - owner_hot
    slot_rank = jnp.sum(before * owner_hot, axis=2)
    target = owner * capacity + slot_rank
    placed = target[:, None, :] == lax.iota(jnp.int32, owners * capacity)[None, :, None]
    buckets = jnp.einsum(
        "sct,std->scd", placed.astype(jnp.bfloat16), slices, preferred_element_type=jnp.float32
    ).astype(jnp.bfloat16)
    bucket_ids = jnp.sum(jnp.where(placed, local[:, None, :] + 1, 0), axis=2) - 1
    buckets = buckets.reshape(seq_count, owners, capacity, slice_width)
    bucket_ids = bucket_ids.reshape(seq_count, owners, capacity)
    arrived, arrived_ids = (
        lax.all_to_all(buckets, "rows", split_axis=1, concat_axis=1, tiled=True),
        lax.all_to_all(bucket_ids, "rows", split_axis=1, concat_axis=1, tiled=True),
    )
    group_size = math.gcd(seq_count, 8)
    grouped_grad = arrived.reshape(
        seq_count // group_size, group_size * owners * capacity, slice_width
    )
    grouped_ids = arrived_ids.reshape(seq_count // group_size, group_size * owners * capacity)

    def add_routed(carried, group_item):
        part_grad, part_ids = group_item
        one_hot = (row_iota[:, None] == part_ids[None, :]).astype(jnp.bfloat16)
        return (carried + jnp.dot(one_hot, part_grad, preferred_element_type=jnp.float32), None)

    start_grad = jnp.zeros((owned_rows, slice_width), jnp.float32)
    row_grad, _ = lax.scan(add_routed, start_grad, (grouped_grad, grouped_ids))
    moment_one_new = 0.9 * moment_one + 0.1 * row_grad
    moment_two_new = 0.999 * moment_two + 0.001 * row_grad * row_grad
    first_fix = 1.0 - 0.9**10
    second_fix = 1.0 - 0.999**10
    update = (
        moment_one_new / first_fix / (jnp.sqrt(moment_two_new / second_fix) + 1e-08) + 0.1 * master
    )
    master_new = master - 0.05 * update
    table_slice = lax.all_gather(master_new.astype(jnp.bfloat16), "rows", axis=0, tiled=True)
    looked_up = jnp.take(table_slice, group_ids, axis=0)
    new_rows = lax.all_to_all(looked_up, "dp", split_axis=0, concat_axis=2, tiled=True)
    return (master_new, moment_one_new, moment_two_new, new_rows)


def solution(mesh):
    return jax.shard_map(
        per_device,
        mesh=mesh,
        in_specs=(
            P(("dp", "rows"), None),
            P(("dp", "rows"), None, None),
            P(("dp", "rows"), None, None),
            P(),
            P("rows", "dp"),
            P("rows", "dp"),
            P("rows", "dp"),
        ),
        out_specs=(
            P("rows", "dp"),
            P("rows", "dp"),
            P("rows", "dp"),
            P(("dp", "rows"), None, None),
        ),
        check_vma=False,
    )
```

profile of v0, /device:TPU:1, one launch (start us, length us, event | category | flops | bytes accessed | tf_op | source)
XLA Modules:
  0.0 313.8 jit_solution(17425573362878609456)
XLA Ops:
  8.6 11.9 %all-to-all-start = ((s32[32,1,128]{2,1,0:T(1,128)}), s32[32,1,128]{2,1,0:T(1,128)S(1)}, u32[]{:S(2)}, u32[]{:S(2)}) async-start(s32[32,1,128]{2,1,0:T(1,128)} %broadcast_in_dim.44), calls=%async_computation | async-start | bytes 32768 | tf_op jit(solution)/shard_map/all_to_all | solution.py:10
  27.1 6.3 %copy.105 = bf16[1,128,5376]{1,0,2:T(2,128)(2,1)S(1)} copy(bf16[1,128,5376]{2,1,0:T(8,128)(2,1)} %fusion.14) | data formatting | bytes 2752512 | tf_op jit(solution)/shard_map/convert_element_type | solution.py:34
  33.9 30.3 %reduce.2 = bf16[5376,128]{1,0:T(8,128)(2,1)} reduce(bf16[5376,1,128]{2,1,0:T(2,128)(2,1)S(1)} %bitcast.66, bf16[]{:T(256)} %broadcast.187), dimensions={1}, to_apply=%bitcast.56.reduce_sub_computation | reduce | bytes 2752514
  64.1 4.0 %reshape.172 = bf16[32,2,10752]{2,1,0:T(2,128)(2,1)} reshape(bf16[5376,128]{1,0:T(8,128)(2,1)} %reduce.2) | data formatting | bytes 2752512
  68.1 9.4 %all-to-all-start.2 = ((bf16[32,2,10752]{2,1,0:T(2,128)(2,1)}), bf16[32,2,10752]{2,1,0:T(2,128)(2,1)S(1)}, u32[]{:S(2)}, u32[]{:S(2)}) async-start(bf16[32,2,10752]{2,1,0:T(2,128)(2,1)} %reshape.172), calls=%async_computation.2 | async-start | bytes 2752512 | tf_op jit(solution)/shard_map/all_to_all | solution.py:43
  77.7 3.3 %fusion.27 = s32[32,128]{0,1:T(8,128)S(1)} fusion(s32[32,128]{0,1:T(8,128)S(1)} %copy.99), kind=kOutput, calls=%fused_computation.37 | output fusion | flops 4386816 | bytes 32768 | tf_op jit(solution)/shard_map/jit(cumsum)/reduce_window_sum | solution.py:51
  83.8 25.5 %all-to-all-done.2 = bf16[32,2,10752]{2,1,0:T(2,128)(2,1)S(1)} async-done(((bf16[32,2,10752]{2,1,0:T(2,128)(2,1)}), bf16[32,2,10752]{2,1,0:T(2,128)(2,1)S(1)}, u32[]{:S(2)}, u32[]{:S(2)}) %all-to-all-start.2) | async-done | bytes 1376288 | tf_op jit(solution)/shard_map/all_to_all | solution.py:43
  110.3 8.1 %all-to-all-start.1 = ((s32[8,1,1024]{2,1,0:T(1,128)}), s32[8,1,1024]{2,1,0:T(1,128)S(1)}, u32[]{:S(2)}, u32[]{:S(2)}) async-start(s32[8,1,1024]{2,1,0:T(1,128)} %reshape.170), calls=%async_computation.1 | async-start | bytes 65536 | tf_op jit(solution)/shard_map/all_to_all | solution.py:63
  118.5 7.8 %reshape.173 = bf16[5376,1,128]{2,1,0:T(2,128)(2,1)S(1)} reshape(bf16[32,2,10752]{2,1,0:T(2,128)(2,1)} %copy-done.2) | data formatting | bytes 2752512
  128.0 4.0 %copy.106 = bf16[32,256,168]{2,1,0:T(8,128)(2,1)} copy(bf16[32,256,168]{1,2,0:T(8,128)(2,1)S(1)} %fusion.26) | data formatting | bytes 5505024 | tf_op jit(solution)/shard_map/convert_element_type | solution.py:57
  132.1 4.8 %copy.107 = bf16[32,8,32,168]{3,2,0,1:T(8,128)(2,1)} copy(bf16[32,8,32,168]{3,2,1,0:T(8,128)(2,1)} %bitcast.65) | data formatting | bytes 5505024 | tf_op jit(solution)/shard_map/reshape | solution.py:59
  136.9 4.8 %all-to-all-start.3 = ((bf16[32,8,32,168]{3,2,0,1:T(8,128)(2,1)}), bf16[32,8,32,168]{3,2,0,1:T(8,128)(2,1)}, u32[]{:S(2)}, u32[]{:S(2)}) async-start(bf16[32,8,32,168]{3,2,0,1:T(8,128)(2,1)} %copy.107), calls=%async_computation.3 | async-start | bytes 8388608 | tf_op jit(solution)/shard_map/all_to_all | solution.py:62
  143.2 47.4 %all-to-all-done.3 = bf16[32,8,32,168]{3,2,0,1:T(8,128)(2,1)} async-done(((bf16[32,8,32,168]{3,2,0,1:T(8,128)(2,1)}), bf16[32,8,32,168]{3,2,0,1:T(8,128)(2,1)}, u32[]{:S(2)}, u32[]{:S(2)}) %all-to-all-start.3) | async-done | bytes 2752544 | tf_op jit(solution)/shard_map/all_to_all | solution.py:62
  190.6 4.8 %copy.108 = bf16[32,8,32,168]{3,2,1,0:T(8,128)(2,1)} copy(bf16[32,8,32,168]{3,2,0,1:T(8,128)(2,1)} %all-to-all-done.3) | data formatting | bytes 5505024 | tf_op jit(solution)/shard_map/all_to_all | solution.py:62
  195.4 13.7 %while.11 = (s32[]{:T(128)}, f32[1024,168]{0,1:T(8,128)S(1)}, s32[4,2048]{1,0:T(4,128)S(1)}, bf16[4,2048,168]{2,1,0:T(8,128)(2,1)}, s32[]{:T(128)}, /*index=5*/s32[]{:T(128)}) while((s32[]{:T(128)}, f32[1024,168]{0,1:T(8,128)S(1)}, s32[4,2048]{1,0:T(4,128)S(1)}, bf16[4,2048,168]{2,1,0:T(8,128)(2,1)}, s32[]{:T(128)}, ...), condition=%wide.region_8.9_spmd.clone, body=%wide.region_7.8_spmd.clone.sunk | while | flops 707084288 | bytes 2450003 | solution.py:77
  195.4 3.5 %fusion.44 = f32[1024,168]{0,1:T(8,128)S(1)} fusion(s32[2048]{0:T(1024)S(1)} %bitcast.77, bf16[4,2048,168]{2,1,0:T(8,128)(2,1)} %get-tuple-element.127, s32[]{:T(128)} %get-tuple-element.118, f32[1024,168]{0,1:T(8,128)S(1)} %get-tuple-element.119, pred[]{:T(512)S(6)} %compare.19), kind=kOutput, calls=%fused_computation.5.clone.1 | convolution fusion | flops 707084288 | bytes 2433537 | tf_op jit(solution)/shard_map/while/body/eval_jaxpr/dot_general | solution.py:74
  198.9 3.3 %fusion.44 = f32[1024,168]{0,1:T(8,128)S(1)} fusion(s32[2048]{0:T(1024)S(1)} %bitcast.77, bf16[4,2048,168]{2,1,0:T(8,128)(2,1)} %get-tuple-element.127, s32[]{:T(128)} %get-tuple-element.118, f32[1024,168]{0,1:T(8,128)S(1)} %get-tuple-element.119, pred[]{:T(512)S(6)} %compare.19), kind=kOutput, calls=%fused_computation.5.clone.1 | convolution fusion | flops 707084288 | bytes 2433537 | tf_op jit(solution)/shard_map/while/body/eval_jaxpr/dot_general | solution.py:74
  202.3 3.3 %fusion.44 = f32[1024,168]{0,1:T(8,128)S(1)} fusion(s32[2048]{0:T(1024)S(1)} %bitcast.77, bf16[4,2048,168]{2,1,0:T(8,128)(2,1)} %get-tuple-element.127, s32[]{:T(128)} %get-tuple-element.118, f32[1024,168]{0,1:T(8,128)S(1)} %get-tuple-element.119, pred[]{:T(512)S(6)} %compare.19), kind=kOutput, calls=%fused_computation.5.clone.1 | convolution fusion | flops 707084288 | bytes 2433537 | tf_op jit(solution)/shard_map/while/body/eval_jaxpr/dot_general | solution.py:74
  205.7 3.3 %fusion.44 = f32[1024,168]{0,1:T(8,128)S(1)} fusion(s32[2048]{0:T(1024)S(1)} %bitcast.77, bf16[4,2048,168]{2,1,0:T(8,128)(2,1)} %get-tuple-element.127, s32[]{:T(128)} %get-tuple-element.118, f32[1024,168]{0,1:T(8,128)S(1)} %get-tuple-element.119, pred[]{:T(512)S(6)} %compare.19), kind=kOutput, calls=%fused_computation.5.clone.1 | convolution fusion | flops 707084288 | bytes 2433537 | tf_op jit(solution)/shard_map/while/body/eval_jaxpr/dot_general | solution.py:74
  210.9 25.4 %all-gather.2.cloned.1.call-done = bf16[8192,168]{0,1:T(8,128)(2,1)} async-done(((bf16[1024,168]{0,1:T(8,128)(2,1)}), bf16[8192,168]{0,1:T(8,128)(2,1)}) %all-gather.2.cloned.1.call-update) | async-done | bytes 2752528 | tf_op jit(solution)/shard_map/all_gather | solution.py:86
  236.3 5.7 %copy.109 = bf16[8192,168]{1,0:T(8,128)(2,1)} copy(bf16[8192,168]{0,1:T(8,128)(2,1)} %all-gather.2.cloned.1.call-done) | data formatting | bytes 5505024 | tf_op jit(solution)/shard_map/all_gather | solution.py:86
  242.0 15.7 %gather_fusion = bf16[4096,168]{1,0:T(8,128)(2,1)S(1)} fusion(bf16[8192,168]{1,0:T(8,128)(2,1)} %copy.109, s32[4096]{0:T(1024)S(1)} %fusion.36), kind=kCustom, calls=%fused_computation | custom fusion | bytes 2768896 | tf_op jit(solution)/shard_map/jit(_take)/gather | solution.py:87
  257.8 2.4 copy.110
  260.4 45.1 %all_to_all.51 = bf16[32,128,168]{1,2,0:T(8,128)(2,1)S(1)} all-to-all(bf16[32,128,168]{1,2,0:T(8,128)(2,1)S(1)} %broadcast_select_fusion), channel_id=1, replica_groups=mesh['dp'=32,'rows'=8] {'dp'}, dimensions={0} | all-to-all | bytes 2752512 | tf_op jit(solution)/shard_map/all_to_all | solution.py:88
  (55 shorter events, 19.2 us)
Async XLA Ops:
  7.2 16.8 %copy-start = (bf16[1,128,5376]{2,1,0:T(8,128)(2,1)S(1)}, bf16[1,128,5376]{2,1,0:T(8,128)(2,1)}, u32[]{:S(2)}) copy-start(bf16[1,128,5376]{2,1,0:T(8,128)(2,1)} %param.11) | copy-start | bytes 4128772
  7.2 16.8 %copy-start.1 = (bf16[1,128,5376]{2,1,0:T(8,128)(2,1)S(1)}, bf16[1,128,5376]{2,1,0:T(8,128)(2,1)}, u32[]{:S(2)}) copy-start(bf16[1,128,5376]{2,1,0:T(8,128)(2,1)} %param.10) | copy-start | bytes 4128772
  7.2 16.8 %copy-start.6 = (f32[5376]{0:T(1024)S(1)}, f32[5376]{0:T(1024)}, u32[]{:S(2)}) copy-start(f32[5376]{0:T(1024)} %param.12) | copy-start | bytes 64516
  8.6 59.5 %all-to-all-start = ((s32[32,1,128]{2,1,0:T(1,128)}), s32[32,1,128]{2,1,0:T(1,128)S(1)}, u32[]{:S(2)}, u32[]{:S(2)}) async-start(s32[32,1,128]{2,1,0:T(1,128)} %broadcast_in_dim.44), calls=%async_computation | async-start | bytes 32768 | tf_op jit(solution)/shard_map/all_to_all | solution.py:10
  68.1 41.1 %all-to-all-start.2 = ((bf16[32,2,10752]{2,1,0:T(2,128)(2,1)}), bf16[32,2,10752]{2,1,0:T(2,128)(2,1)S(1)}, u32[]{:S(2)}, u32[]{:S(2)}) async-start(bf16[32,2,10752]{2,1,0:T(2,128)(2,1)} %reshape.172), calls=%async_computation.2 | async-start | bytes 2752512 | tf_op jit(solution)/shard_map/all_to_all | solution.py:43
  109.2 1.1 copy-start.2
  110.3 26.5 %all-to-all-start.1 = ((s32[8,1,1024]{2,1,0:T(1,128)}), s32[8,1,1024]{2,1,0:T(1,128)S(1)}, u32[]{:S(2)}, u32[]{:S(2)}) async-start(s32[8,1,1024]{2,1,0:T(1,128)} %reshape.170), calls=%async_computation.1 | async-start | bytes 65536 | tf_op jit(solution)/shard_map/all_to_all | solution.py:63
  136.9 53.7 %all-to-all-start.3 = ((bf16[32,8,32,168]{3,2,0,1:T(8,128)(2,1)}), bf16[32,8,32,168]{3,2,0,1:T(8,128)(2,1)}, u32[]{:S(2)}, u32[]{:S(2)}) async-start(bf16[32,8,32,168]{3,2,0,1:T(8,128)(2,1)} %copy.107), calls=%async_computation.3 | async-start | bytes 8388608 | tf_op jit(solution)/shard_map/all_to_all | solution.py:62
  141.7 94.6 %all-gather.2.cloned.1.call-start = ((), (), s32[]{:S(2)}) async-start(), calls=%async_computation.5 | async-start | bytes 3096576 | tf_op jit(solution)/shard_map/all_gather | solution.py:86
  195.4 13.7 %copy-start.3 = (f32[1024,168]{0,1:T(8,128)S(1)}, f32[1024,168]{0,1:T(8,128)}, u32[]{:S(2)}) copy-start(f32[1024,168]{0,1:T(8,128)} %param.13) | copy-start | bytes 2064388
  195.4 13.7 %copy-start.4 = (f32[1024,168]{0,1:T(8,128)S(1)}, f32[1024,168]{0,1:T(8,128)}, u32[]{:S(2)}) copy-start(f32[1024,168]{0,1:T(8,128)} %param.14) | copy-start | bytes 2064388
  195.4 13.7 %copy-start.5 = (f32[1024,168]{0,1:T(8,128)S(1)}, f32[1024,168]{0,1:T(8,128)}, u32[]{:S(2)}) copy-start(f32[1024,168]{0,1:T(8,128)} %param.15) | copy-start | bytes 2064388
Sparse Core Ops, SparseCore 0:
  211.0 25.2 all-gather.1
where the time goes:
time: 315 us; the launch traced here: 314 us
  waiting for transfers between devices  98.2 us (31%)
  local copies, waits for them, and re-layouts  62.4 us (20%)
  blocking collectives  45.1 us (14%)
  other arithmetic  44.5 us (14%)
  starting transfers between devices  34.2 us (11%)
  matrix products  15 us (5%)
  between operations  14.3 us (5%)
    all_to_all x1, waiting for transfers between devices, per_device(): lax.all_to_all(buckets, 'rows', split_axis=1, concat_axis=1, tiled=True)  47.4 us
    all_to_all x1, blocking collectives, per_device(): lax.all_to_all(looked_up, 'dp', split_axis=0, concat_axis=2, tiled=True)  45.1 us
    unnamed x2, other arithmetic  30.3 us
    all_to_all x1, waiting for transfers between devices, per_device(): lax.all_to_all(row_input, 'dp', split_axis=2, concat_axis=0, tiled=True)  25.5 us
    all_gather x1, waiting for transfers between devices, per_device(): lax.all_gather(master_new.astype(jnp.bfloat16), 'rows', axis=0, tiled=True)  25.4 us
    gather x2, local copies, waits for them, and re-layouts, per_device(): looked_up = jnp.take(table_slice, group_ids, axis=0)  18.2 us
    unnamed x21, local copies, waits for them, and re-layouts  15.9 us
    dot_general x4, matrix products, add_routed(): jnp.dot(one_hot, part_grad, preferred_element_type=jnp.float32)  13.5 us
  transfers between devices with their start and end apart: 5, of which 3 were waited for; matrix products, arithmetic and copies ran while one was open for 23% of the time, Pallas kernels for 0%

commit v1 on v0

--- a/solution.py
+++ b/solution.py
@@ -3,6 +3,29 @@
 import jax.numpy as jnp
 from jax import lax
 from jax.sharding import PartitionSpec as P
+
+
+def cut_along(x, dim, devices):
+    before, after = (x.shape[:dim], x.shape[dim + 1 :])
+    return jnp.moveaxis(x.reshape(*before, devices, -1, *after), dim, 0)
+
+
+def laid_out(blocks, dim):
+    blocks = jnp.moveaxis(blocks, 0, dim)
+    shape = blocks.shape
+    return blocks.reshape(*shape[:dim], shape[dim] * shape[dim + 1], *shape[dim + 2 :])
+
+
+def sent_to_each(x, axis, split_dim, concat_dim):
+    length, place = (lax.axis_size(axis), lax.axis_index(axis))
+    tiles = cut_along(x, split_dim, length)
+    out = tiles
+    for hop in range(1, length):
+        target, source = ((place + hop) % length, (place - hop) % length)
+        sent = lax.dynamic_index_in_dim(tiles, target, 0)
+        partner_block = lax.ppermute(sent, axis, [(i, (i + hop) % length) for i in range(length)])
+        out = lax.dynamic_update_slice_in_dim(out, partner_block, source, axis=0)
+    return laid_out(out, concat_dim)
 
 
 def from_everyone(x, axis):
@@ -59,7 +82,7 @@
     buckets = buckets.reshape(seq_count, owners, capacity, slice_width)
     bucket_ids = bucket_ids.reshape(seq_count, owners, capacity)
     arrived, arrived_ids = (
-        lax.all_to_all(buckets, "rows", split_axis=1, concat_axis=1, tiled=True),
+        sent_to_each(buckets, "rows", 1, 1),
         lax.all_to_all(bucket_ids, "rows", split_axis=1, concat_axis=1, tiled=True),
     )
     group_size = math.gcd(seq_count, 8)

time: 315 us -> 328 us (1.041)
  waiting for transfers between devices: 98.2 us -> 107 us
    all_to_all x1 -> x0, waiting for transfers between devices: 47.4 us -> none  [per_device(): lax.all_to_all(buckets, 'rows', split_axis=1, concat_axis=1, tiled=True)]
    ppermute x0 -> x7, waiting for transfers between devices: none -> 28.7 us  [sent_to_each(): lax.ppermute(sent, axis, [(i, (i + hop) % length) for i in range(length)])]
    all_to_all x1, waiting for transfers between devices: 0.01 us -> 23.5 us  [per_device(): lax.all_to_all(bucket_ids, 'rows', split_axis=1, concat_axis=1, tiled=True)]
    ppermute x0 -> x7, starting transfers between devices: none -> 11.6 us  [sent_to_each(): lax.ppermute(sent, axis, [(i, (i + hop) % length) for i in range(length)])]
    dynamic_update_slice x0 -> x7, local copies, waits for them, and re-layouts: none -> 9.19 us  [sent_to_each(): out = lax.dynamic_update_slice_in_dim(out, partner_block, source, axis=0)]
    all_to_all x1, starting transfers between devices: 8.14 us -> 3.29 us  [per_device(): lax.all_to_all(bucket_ids, 'rows', split_axis=1, concat_axis=1, tiled=True)]
    all_to_all x1 -> x0, starting transfers between devices: 4.8 us -> none  [per_device(): lax.all_to_all(buckets, 'rows', split_axis=1, concat_axis=1, tiled=True)]
    all_to_all x1 -> x0, local copies, waits for them, and re-layouts: 4.8 us -> none  [per_device(): lax.all_to_all(buckets, 'rows', split_axis=1, concat_axis=1, tiled=True)]
  transfers between devices with their start and end apart: 5 -> 11, of which waited for: 3 -> 6; matrix products, arithmetic and copies ran while one was open for 23% -> 19% of each run, Pallas kernels for 0% -> 0%
where the time goes in v1:
time: 328 us; the launch traced here: 327 us
  waiting for transfers between devices  107 us (33%)
  local copies, waits for them, and re-layouts  64.3 us (20%)
  blocking collectives  45.1 us (14%)
  other arithmetic  44.5 us (14%)
  starting transfers between devices  36.3 us (11%)
  matrix products  15 us (5%)
  between operations  14.5 us (4%)
    all_to_all x1, blocking collectives, per_device(): lax.all_to_all(looked_up, 'dp', split_axis=0, concat_axis=2, tiled=True)  45.1 us
    unnamed x2, other arithmetic  30.3 us
    ppermute x7, waiting for transfers between devices, sent_to_each(): lax.ppermute(sent, axis, [(i, (i + hop) % length) for i in range(length)])  28.7 us
    all_to_all x1, waiting for transfers between devices, per_device(): lax.all_to_all(row_input, 'dp', split_axis=2, concat_axis=0, tiled=True)  28 us
    all_gather x1, waiting for transfers between devices, per_device(): lax.all_gather(master_new.astype(jnp.bfloat16), 'rows', axis=0, tiled=True)  26.9 us
    all_to_all x1, waiting for transfers between devices, per_device(): lax.all_to_all(bucket_ids, 'rows', split_axis=1, concat_axis=1, tiled=True)  23.5 us
    gather x2, local copies, waits for them, and re-layouts, per_device(): looked_up = jnp.take(table_slice, group_ids, axis=0)  18.2 us
    unnamed x19, local copies, waits for them, and re-layouts  14.9 us
  transfers between devices with their start and end apart: 11, of which 6 were waited for; matrix products, arithmetic and copies ran while one was open for 19% of the time, Pallas kernels for 0%

profile of v1, /device:TPU:1, one launch (start us, length us, event | category | flops | bytes accessed | tf_op | source)
XLA Modules:
  0.0 326.9 jit_solution(6724296511437648638)
XLA Ops:
  8.6 11.9 %all-to-all-start = ((s32[32,1,128]{2,1,0:T(1,128)}), s32[32,1,128]{2,1,0:T(1,128)S(1)}, u32[]{:S(2)}, u32[]{:S(2)}) async-start(s32[32,1,128]{2,1,0:T(1,128)} %broadcast_in_dim.44), calls=%async_computation | async-start | bytes 32768 | tf_op jit(solution)/shard_map/all_to_all | solution.py:33
  27.1 6.3 %copy.102 = bf16[1,128,5376]{1,0,2:T(2,128)(2,1)S(1)} copy(bf16[1,128,5376]{2,1,0:T(8,128)(2,1)} %fusion.14) | data formatting | bytes 2752512 | tf_op jit(solution)/shard_map/convert_element_type | solution.py:57
  33.9 30.3 %reduce.2 = bf16[5376,128]{1,0:T(8,128)(2,1)} reduce(bf16[5376,1,128]{2,1,0:T(2,128)(2,1)S(1)} %bitcast.86, bf16[]{:T(256)} %broadcast.201), dimensions={1}, to_apply=%bitcast.74.reduce_sub_computation | reduce | bytes 2752514
  64.1 4.0 %reshape.171 = bf16[32,2,10752]{2,1,0:T(2,128)(2,1)} reshape(bf16[5376,128]{1,0:T(8,128)(2,1)} %reduce.2) | data formatting | bytes 2752512
  68.1 9.5 %all-to-all-start.2 = ((bf16[32,2,10752]{2,1,0:T(2,128)(2,1)}), bf16[32,2,10752]{2,1,0:T(2,128)(2,1)}, u32[]{:S(2)}, u32[]{:S(2)}) async-start(bf16[32,2,10752]{2,1,0:T(2,128)(2,1)} %reshape.171), calls=%async_computation.2 | async-start | bytes 2752512 | tf_op jit(solution)/shard_map/all_to_all | solution.py:66
  78.0 3.3 %fusion.27 = s32[32,128]{0,1:T(8,128)S(1)} fusion(s32[32,128]{0,1:T(8,128)S(1)} %copy.96), kind=kOutput, calls=%fused_computation.37 | output fusion | flops 4386816 | bytes 32768 | tf_op jit(solution)/shard_map/jit(cumsum)/reduce_window_sum | solution.py:74
  81.5 28.0 %all-to-all-done.2 = bf16[32,2,10752]{2,1,0:T(2,128)(2,1)} async-done(((bf16[32,2,10752]{2,1,0:T(2,128)(2,1)}), bf16[32,2,10752]{2,1,0:T(2,128)(2,1)}, u32[]{:S(2)}, u32[]{:S(2)}) %all-to-all-start.2) | async-done | bytes 1376288 | tf_op jit(solution)/shard_map/all_to_all | solution.py:66
  109.5 7.8 %reshape.172 = bf16[5376,1,128]{2,1,0:T(2,128)(2,1)S(1)} reshape(bf16[32,2,10752]{2,1,0:T(2,128)(2,1)} %all-to-all-done.2) | data formatting | bytes 2752512
  119.1 4.0 %copy.103 = bf16[32,256,168]{2,1,0:T(8,128)(2,1)} copy(bf16[32,256,168]{1,2,0:T(8,128)(2,1)S(1)} %fusion.26) | data formatting | bytes 5505024 | tf_op jit(solution)/shard_map/convert_element_type | solution.py:80
  123.1 3.4 %dynamic-slice_bitcast_fusion = (bf16[1,32,1,32,168]{4,3,0,1,2:T(8,128)(2,1)S(1)}, bf16[1,32,1,32,168]{4,3,0,1,2:T(8,128)(2,1)S(1)}, bf16[1,32,1,32,168]{4,3,0,1...) fusion(bf16[32,8,1,32,168]{4,3,1,0,2:T(8,128)(2,1)} %bitcast.83, ...), kind=kLoop, calls=%fused_computation.46 | loop fusion | bytes 4816924 | tf_op jit(solution)/shard_map/jit(dynamic_index_in_dim)/dynamic_slice | solution.py:25
  126.5 4.7 %collective-permute-start = (bf16[1,32,1,32,168]{4,3,0,1,2:T(8,128)(2,1)}, bf16[1,32,1,32,168]{4,3,0,1,2:T(8,128)(2,1)}, u32[]{:S(2)}, u32[]{:S(2)}) collective-permute-start(bf16[1,32,1,32,168]{4,3,0,1,2:T(8,128)(2,1)} %get-tuple-element.89), channel_id=1, source_target_pairs={{0,1},{1,2},{2,3},{3,4},{4,5},{5,6},{6,7},{7,0},{8,9},{9,10},{10,1... | collective-permute-start | bytes 1032200 | tf_op jit(solution)/shard_map/ppermute | solution.py:26
  140.2 23.5 %all-to-all-done.1 = s32[8,1,1024]{2,1,0:T(1,128)S(1)} async-done(((s32[8,1,1024]{2,1,0:T(1,128)}), s32[8,1,1024]{2,1,0:T(1,128)S(1)}, u32[]{:S(2)}, u32[]{:S(2)}) %all-to-all-start.1) | async-done | bytes 32800 | tf_op jit(solution)/shard_map/all_to_all | solution.py:86
  174.9 5.0 %collective-permute-done.3 = bf16[1,32,1,32,168]{4,3,0,1,2:T(8,128)(2,1)S(1)} collective-permute-done((bf16[1,32,1,32,168]{4,3,0,1,2:T(8,128)(2,1)S(1)}, bf16[1,32,1,32,168]{4,3,0,1,2:T(8,128)(2,1)S(1)}, u32[]{:S(2)}, u32[]{:S(2)}) %collective-permute-start.3) | collective-permute-done | bytes 344096 | tf_op jit(solution)/shard_map/ppermute | solution.py:26
  180.7 13.3 %collective-permute-done.4 = bf16[1,32,1,32,168]{4,3,0,1,2:T(8,128)(2,1)S(1)} collective-permute-done((bf16[1,32,1,32,168]{4,3,0,1,2:T(8,128)(2,1)S(1)}, bf16[1,32,1,32,168]{4,3,0,1,2:T(8,128)(2,1)S(1)}, u32[]{:S(2)}, u32[]{:S(2)}) %collective-permute-start.4) | collective-permute-done | bytes 344096 | tf_op jit(solution)/shard_map/ppermute | solution.py:26
  194.9 10.4 %collective-permute-done.5 = bf16[1,32,1,32,168]{4,3,0,1,2:T(8,128)(2,1)S(1)} collective-permute-done((bf16[1,32,1,32,168]{4,3,0,1,2:T(8,128)(2,1)S(1)}, bf16[1,32,1,32,168]{4,3,0,1,2:T(8,128)(2,1)S(1)}, u32[]{:S(2)}, u32[]{:S(2)}) %collective-permute-start.5) | collective-permute-done | bytes 344096 | tf_op jit(solution)/shard_map/ppermute | solution.py:26
  207.0 13.6 %while.11 = (s32[]{:T(128)}, f32[1024,168]{0,1:T(8,128)S(1)}, s32[4,2048]{1,0:T(4,128)S(1)}, bf16[4,2048,168]{2,1,0:T(8,128)(2,1)}, s32[]{:T(128)}, /*index=5*/s32[]{:T(128)}) while((s32[]{:T(128)}, f32[1024,168]{0,1:T(8,128)S(1)}, s32[4,2048]{1,0:T(4,128)S(1)}, bf16[4,2048,168]{2,1,0:T(8,128)(2,1)}, s32[]{:T(128)}, ...), condition=%wide.region_8.9_spmd.clone, body=%wide.region_7.8_spmd.clone.sunk | while | flops 707084288 | bytes 2450003 | solution.py:100
  207.0 3.5 %fusion.44 = f32[1024,168]{0,1:T(8,128)S(1)} fusion(s32[2048]{0:T(1024)S(1)} %bitcast.96, bf16[4,2048,168]{2,1,0:T(8,128)(2,1)} %get-tuple-element.134, s32[]{:T(128)} %get-tuple-element.125, f32[1024,168]{0,1:T(8,128)S(1)} %get-tuple-element.126, pred[]{:T(512)S(6)} %compare.33), kind=kOutput, calls=%fused_computation.5.clone.1 | convolution fusion | flops 707084288 | bytes 2433537 | tf_op jit(solution)/shard_map/while/body/eval_jaxpr/dot_general | solution.py:97
  210.6 3.3 %fusion.44 = f32[1024,168]{0,1:T(8,128)S(1)} fusion(s32[2048]{0:T(1024)S(1)} %bitcast.96, bf16[4,2048,168]{2,1,0:T(8,128)(2,1)} %get-tuple-element.134, s32[]{:T(128)} %get-tuple-element.125, f32[1024,168]{0,1:T(8,128)S(1)} %get-tuple-element.126, pred[]{:T(512)S(6)} %compare.33), kind=kOutput, calls=%fused_computation.5.clone.1 | convolution fusion | flops 707084288 | bytes 2433537 | tf_op jit(solution)/shard_map/while/body/eval_jaxpr/dot_general | solution.py:97
  213.9 3.3 %fusion.44 = f32[1024,168]{0,1:T(8,128)S(1)} fusion(s32[2048]{0:T(1024)S(1)} %bitcast.96, bf16[4,2048,168]{2,1,0:T(8,128)(2,1)} %get-tuple-element.134, s32[]{:T(128)} %get-tuple-element.125, f32[1024,168]{0,1:T(8,128)S(1)} %get-tuple-element.126, pred[]{:T(512)S(6)} %compare.33), kind=kOutput, calls=%fused_computation.5.clone.1 | convolution fusion | flops 707084288 | bytes 2433537 | tf_op jit(solution)/shard_map/while/body/eval_jaxpr/dot_general | solution.py:97
  217.3 3.3 %fusion.44 = f32[1024,168]{0,1:T(8,128)S(1)} fusion(s32[2048]{0:T(1024)S(1)} %bitcast.96, bf16[4,2048,168]{2,1,0:T(8,128)(2,1)} %get-tuple-element.134, s32[]{:T(128)} %get-tuple-element.125, f32[1024,168]{0,1:T(8,128)S(1)} %get-tuple-element.126, pred[]{:T(512)S(6)} %compare.33), kind=kOutput, calls=%fused_computation.5.clone.1 | convolution fusion | flops 707084288 | bytes 2433537 | tf_op jit(solution)/shard_map/while/body/eval_jaxpr/dot_general | solution.py:97
  222.6 26.9 %all-gather.2.cloned.1.call-done = bf16[8192,168]{0,1:T(8,128)(2,1)} async-done(((bf16[1024,168]{0,1:T(8,128)(2,1)}), bf16[8192,168]{0,1:T(8,128)(2,1)}) %all-gather.2.cloned.1.call-update) | async-done | bytes 2752528 | tf_op jit(solution)/shard_map/all_gather | solution.py:109
  249.4 5.7 %copy.104 = bf16[8192,168]{1,0:T(8,128)(2,1)} copy(bf16[8192,168]{0,1:T(8,128)(2,1)} %all-gather.2.cloned.1.call-done) | data formatting | bytes 5505024 | tf_op jit(solution)/shard_map/all_gather | solution.py:109
  255.2 15.7 %gather_fusion = bf16[4096,168]{1,0:T(8,128)(2,1)S(1)} fusion(bf16[8192,168]{1,0:T(8,128)(2,1)} %copy.104, s32[4096]{0:T(1024)S(1)} %fusion.36), kind=kCustom, calls=%fused_computation | custom fusion | bytes 2768896 | tf_op jit(solution)/shard_map/jit(_take)/gather | solution.py:110
  273.5 45.1 %all_to_all.46 = bf16[32,128,168]{1,2,0:T(8,128)(2,1)S(1)} all-to-all(bf16[32,128,168]{1,2,0:T(8,128)(2,1)S(1)} %broadcast_select_fusion), channel_id=1, replica_groups=mesh['dp'=32,'rows'=8] {'dp'}, dimensions={0} | all-to-all | bytes 2752512 | tf_op jit(solution)/shard_map/all_to_all | solution.py:111
  (71 shorter events, 40.0 us)
Async XLA Ops:
  7.2 16.8 %copy-start = (bf16[1,128,5376]{2,1,0:T(8,128)(2,1)S(1)}, bf16[1,128,5376]{2,1,0:T(8,128)(2,1)}, u32[]{:S(2)}) copy-start(bf16[1,128,5376]{2,1,0:T(8,128)(2,1)} %param.11) | copy-start | bytes 4128772
  7.2 16.8 %copy-start.1 = (bf16[1,128,5376]{2,1,0:T(8,128)(2,1)S(1)}, bf16[1,128,5376]{2,1,0:T(8,128)(2,1)}, u32[]{:S(2)}) copy-start(bf16[1,128,5376]{2,1,0:T(8,128)(2,1)} %param.10) | copy-start | bytes 4128772
  7.2 16.8 %copy-start.5 = (f32[5376]{0:T(1024)S(1)}, f32[5376]{0:T(1024)}, u32[]{:S(2)}) copy-start(f32[5376]{0:T(1024)} %param.12) | copy-start | bytes 64516
  8.6 59.5 %all-to-all-start = ((s32[32,1,128]{2,1,0:T(1,128)}), s32[32,1,128]{2,1,0:T(1,128)S(1)}, u32[]{:S(2)}, u32[]{:S(2)}) async-start(s32[32,1,128]{2,1,0:T(1,128)} %broadcast_in_dim.44), calls=%async_computation | async-start | bytes 32768 | tf_op jit(solution)/shard_map/all_to_all | solution.py:33
  68.1 41.4 %all-to-all-start.2 = ((bf16[32,2,10752]{2,1,0:T(2,128)(2,1)}), bf16[32,2,10752]{2,1,0:T(2,128)(2,1)}, u32[]{:S(2)}, u32[]{:S(2)}) async-start(bf16[32,2,10752]{2,1,0:T(2,128)(2,1)} %reshape.171), calls=%async_computation.2 | async-start | bytes 2752512 | tf_op jit(solution)/shard_map/all_to_all | solution.py:66
  126.5 40.7 %collective-permute-start = (bf16[1,32,1,32,168]{4,3,0,1,2:T(8,128)(2,1)}, bf16[1,32,1,32,168]{4,3,0,1,2:T(8,128)(2,1)}, u32[]{:S(2)}, u32[]{:S(2)}) collective-permute-start(bf16[1,32,1,32,168]{4,3,0,1,2:T(8,128)(2,1)} %get-tuple-element.89), channel_id=1, source_target_pairs={{0,1},{1,2},{2,3},{3,4},{4,5},{5,6},{6,7},{7,0},{8,9},{9,10},{10,1... | collective-permute-start | bytes 1032200 | tf_op jit(solution)/shard_map/ppermute | solution.py:26
  132.8 38.2 %collective-permute-start.1 = (bf16[1,32,1,32,168]{4,3,0,1,2:T(8,128)(2,1)}, bf16[1,32,1,32,168]{4,3,0,1,2:T(8,128)(2,1)}, u32[]{:S(2)}, u32[]{:S(2)}) collective-permute-start(bf16[1,32,1,32,168]{4,3,0,1,2:T(8,128)(2,1)} %get-tuple-element.88), channel_id=1, source_target_pairs={{0,2},{1,3},{2,4},{3,5},{4,6},{5,7},{6,0},{7,1},{8,10},{9,11},{10,... | collective-permute-start | bytes 1032200 | tf_op jit(solution)/shard_map/ppermute | solution.py:26
  134.2 38.7 %collective-permute-start.2 = (bf16[1,32,1,32,168]{4,3,0,1,2:T(8,128)(2,1)}, bf16[1,32,1,32,168]{4,3,0,1,2:T(8,128)(2,1)}, u32[]{:S(2)}, u32[]{:S(2)}) collective-permute-start(bf16[1,32,1,32,168]{4,3,0,1,2:T(8,128)(2,1)} %get-tuple-element.87), channel_id=1, source_target_pairs={{0,3},{1,4},{2,5},{3,6},{4,7},{5,0},{6,1},{7,2},{8,11},{9,12},{10,... | collective-permute-start | bytes 1032200 | tf_op jit(solution)/shard_map/ppermute | solution.py:26
  136.7 27.0 %all-to-all-start.1 = ((s32[8,1,1024]{2,1,0:T(1,128)}), s32[8,1,1024]{2,1,0:T(1,128)S(1)}, u32[]{:S(2)}, u32[]{:S(2)}) async-start(s32[8,1,1024]{2,1,0:T(1,128)} %reshape.169), calls=%async_computation.1 | async-start | bytes 65536 | tf_op jit(solution)/shard_map/all_to_all | solution.py:86
  140.0 109.5 %all-gather.2.cloned.1.call-start = ((), (), s32[]{:S(2)}) async-start(), calls=%async_computation.4 | async-start | bytes 3096576 | tf_op jit(solution)/shard_map/all_gather | solution.py:109
  165.2 14.7 %collective-permute-start.3 = (bf16[1,32,1,32,168]{4,3,0,1,2:T(8,128)(2,1)S(1)}, bf16[1,32,1,32,168]{4,3,0,1,2:T(8,128)(2,1)S(1)}, u32[]{:S(2)}, u32[]{:S(2)}) collective-permute-start(bf16[1,32,1,32,168]{4,3,0,1,2:T(8,128)(2,1)S(1)} %get-tuple-element.86), channel_id=1, source_target_pairs={{0,4},{1,5},{2,6},{3,7},{4,0},{5,1},{6,2},{7,3},{8,12},{9,13},{10,... | collective-permute-start | bytes 1032200 | tf_op jit(solution)/shard_map/ppermute | solution.py:26
  165.7 28.4 %collective-permute-start.4 = (bf16[1,32,1,32,168]{4,3,0,1,2:T(8,128)(2,1)S(1)}, bf16[1,32,1,32,168]{4,3,0,1,2:T(8,128)(2,1)S(1)}, u32[]{:S(2)}, u32[]{:S(2)}) collective-permute-start(bf16[1,32,1,32,168]{4,3,0,1,2:T(8,128)(2,1)S(1)} %get-tuple-element.85), channel_id=1, source_target_pairs={{0,5},{1,6},{2,7},{3,0},{4,1},{5,2},{6,3},{7,4},{8,13},{9,14},{10,... | collective-permute-start | bytes 1032200 | tf_op jit(solution)/shard_map/ppermute | solution.py:26
  167.2 38.1 %collective-permute-start.5 = (bf16[1,32,1,32,168]{4,3,0,1,2:T(8,128)(2,1)S(1)}, bf16[1,32,1,32,168]{4,3,0,1,2:T(8,128)(2,1)S(1)}, u32[]{:S(2)}, u32[]{:S(2)}) collective-permute-start(bf16[1,32,1,32,168]{4,3,0,1,2:T(8,128)(2,1)S(1)} %get-tuple-element.84), channel_id=1, source_target_pairs={{0,6},{1,7},{2,0},{3,1},{4,2},{5,3},{6,4},{7,5},{8,14},{9,15},{10,... | collective-permute-start | bytes 1032200 | tf_op jit(solution)/shard_map/ppermute | solution.py:26
  171.0 35.2 %collective-permute-start.6 = (bf16[1,32,1,32,168]{4,3,0,1,2:T(8,128)(2,1)S(1)}, bf16[1,32,1,32,168]{4,3,0,1,2:T(8,128)(2,1)S(1)}, u32[]{:S(2)}, u32[]{:S(2)}) collective-permute-start(bf16[1,32,1,32,168]{4,3,0,1,2:T(8,128)(2,1)S(1)} %get-tuple-element.83), channel_id=1, source_target_pairs={{0,7},{1,0},{2,1},{3,2},{4,3},{5,4},{6,5},{7,6},{8,15},{9,8},{10,9... | collective-permute-start | bytes 1032200 | tf_op jit(solution)/shard_map/ppermute | solution.py:26
  207.0 13.7 %copy-start.2 = (f32[1024,168]{0,1:T(8,128)S(1)}, f32[1024,168]{0,1:T(8,128)}, u32[]{:S(2)}) copy-start(f32[1024,168]{0,1:T(8,128)} %param.13) | copy-start | bytes 2064388
  207.0 13.7 %copy-start.3 = (f32[1024,168]{0,1:T(8,128)S(1)}, f32[1024,168]{0,1:T(8,128)}, u32[]{:S(2)}) copy-start(f32[1024,168]{0,1:T(8,128)} %param.14) | copy-start | bytes 2064388
  207.0 13.7 %copy-start.4 = (f32[1024,168]{0,1:T(8,128)S(1)}, f32[1024,168]{0,1:T(8,128)}, u32[]{:S(2)}) copy-start(f32[1024,168]{0,1:T(8,128)} %param.15) | copy-start | bytes 2064388
Sparse Core Ops, SparseCore 0:
  222.6 26.7 all-gather.1
